TPU v7x, 32 devices: a whole 2x2x4 slice. The times are simulated.
32 devices in a mesh: row: 8 (over y, x, core), col: 4 (over z).
Axes of the slice: x: 2, y: 2, z: 4, core: 2. Of those that a mesh axis runs over, the one named last changes fastest.
Arguments:
- ancestor: float32 [9, 9, 512, 512], P(None, None, 'row', 'col'), may hold values from -1 to 4, as said below
- inverse_first: float32 [2, 2, 512, 512], P(None, None, 'row', 'col'), may hold values from -1 to 2, as said below
- panel_first: float32 [1536, 2, 512], P('row', None, 'col'), may hold values from -0.15625 to 0.15625
- structure_first: int32 [1536], replicated, may hold values from 0 to 4607, as said below
- inverse_second: float32 [1, 1, 512, 512], P(None, None, 'row', 'col'), may hold values from -1 to 2, as said below
- panel_second: float32 [1536, 1, 512], P('row', None, 'col'), may hold values from -0.15625 to 0.15625
- structure_second: int32 [1536], replicated, may hold values from 0 to 5631, as said below
Outputs:
- row_first: float32 [2, 11, 512, 512], P(None, None, 'row', 'col')
- row_second: float32 [1, 12, 512, 512], P(None, None, 'row', 'col')
Inputs may be any that keep to these rules, and one draw needn't show every extreme that they name: `ancestor`: symmetric and positive definite as a matrix. `inverse_first`: symmetric and positive definite as a matrix. `inverse_second`: symmetric and positive definite as a matrix. `structure_first`: entries are distinct; every aligned group of 16 ancestor rows holds at most 6 entries, and some group holds exactly 6. `structure_second`: entries are distinct; every aligned group of 16 ancestor rows holds at most 6 entries, and some group holds exactly 6.
All inputs are finite; a program needn't handle non-finite values.
Results may differ from a plain program's by a relative error of at most 0.000075.
Values sent between devices are 32-bit elements; how exact they have to be, the bound alone decides.
A program may use at most 128 MiB of HBM per device.

v0:
```python
import jax
import jax.numpy as jnp
from jax import lax
from jax.sharding import PartitionSpec as P

TILE = 512
GRAIN = 16
CAP = 6


def open_packed(packed, row_height, col_width):
    return packed.reshape(packed.shape[0], packed.shape[1], row_height, col_width)


def close_packed(tiles):
    depth = tiles.shape[2] * tiles.shape[3] // 128
    return tiles.reshape(tiles.shape[0], tiles.shape[1], depth, 128)


def expand_panel(panel_part, structure, tile_count):
    gathered = lax.all_gather(panel_part, "row", axis=0, tiled=True)
    flattened = gathered.reshape(gathered.shape[0], gathered.shape[1] * gathered.shape[2])
    expanded = (
        jnp.zeros((tile_count * TILE, flattened.shape[1]), jnp.float32).at[structure].set(flattened)
    )
    return expanded.reshape(tile_count, TILE, gathered.shape[1], gathered.shape[2])


def pick_slots(row_marks, tile_count, start, width):
    window = lax.dynamic_slice_in_dim(row_marks.reshape(tile_count, TILE), start, width, 1)
    groups = width // GRAIN
    ranking = window.reshape(tile_count, groups, GRAIN) * (
        GRAIN - jnp.arange(GRAIN, dtype=jnp.int32)
    )
    chosen = lax.top_k(ranking, CAP)[1]
    chosen = chosen + (jnp.arange(groups, dtype=jnp.int32) * GRAIN)[None, :, None]
    return chosen.reshape(tile_count, groups * CAP)


def take_along(source, slots, take_axis, tile_axis):
    return jax.vmap(
        lambda portion, picked: jnp.take(portion, picked, axis=take_axis),
        in_axes=(tile_axis, 0),
        out_axes=tile_axis,
    )(source, slots)


def sweep_step(blocks, inverse, panel_part, structure):
    tile_count = blocks.shape[0]
    row_height = blocks.shape[2]
    col_width = blocks.shape[3]
    new_tiles = inverse.shape[0]
    row_index = lax.axis_index("row")
    col_index = lax.axis_index("col")
    spread = expand_panel(panel_part, structure, tile_count)
    own_rows = lax.dynamic_slice_in_dim(spread, row_index * row_height, row_height, 1)
    row_panel = lax.all_gather(own_rows, "col", axis=3, tiled=True)
    regrouped = spread.reshape(tile_count, TILE // col_width, col_width, new_tiles, 1, col_width)
    received = lax.all_to_all(regrouped, "col", split_axis=1, concat_axis=4, tiled=True)
    col_panel = received.reshape(tile_count, col_width, new_tiles, TILE)
    row_marks = jnp.zeros((tile_count * TILE,), jnp.int32).at[structure].set(1)
    col_slots = pick_slots(row_marks, tile_count, col_index * col_width, col_width)
    row_slots = pick_slots(row_marks, tile_count, row_index * row_height, row_height)
    kept_cols = take_along(blocks, col_slots, 2, 1)
    compact_cols = take_along(col_panel, col_slots, 0, 0)
    compact_rows = take_along(row_panel, row_slots, 0, 0)
    image_terms = jnp.einsum(
        "ijak,jknw->inaw", kept_cols, compact_cols, precision=lax.Precision.HIGHEST
    )
    image = lax.psum_scatter(image_terms, "col", scatter_dimension=3, tiled=True)
    kept_rows = take_along(blocks, row_slots, 1, 0)
    cross_terms = jnp.einsum(
        "iakw,ijab->kjwb", compact_rows, kept_rows, precision=lax.Precision.HIGHEST
    )
    cross = lax.psum_scatter(cross_terms, "row", scatter_dimension=2, tiled=True)
    image_kept = take_along(image, row_slots, 1, 0)
    diag_terms = jnp.einsum(
        "iakw,imac->kmwc", compact_rows, image_kept, precision=lax.Precision.HIGHEST
    )
    diagonal = inverse + lax.psum_scatter(diag_terms, "row", scatter_dimension=2, tiled=True)
    row_tiles = jnp.concatenate([-cross, diagonal], axis=1)
    upper_tiles = jnp.concatenate([blocks, -image], axis=1)
    frontier = jnp.concatenate([upper_tiles, row_tiles], axis=0)
    return (row_tiles, frontier)


def on_device(
    ancestor,
    inverse_first,
    panel_first,
    structure_first,
    inverse_second,
    panel_second,
    structure_second,
):
    row_height = TILE // lax.axis_size("row")
    col_width = TILE // lax.axis_size("col")
    blocks = open_packed(ancestor, row_height, col_width)
    first_diag = open_packed(inverse_first, row_height, col_width)
    second_diag = open_packed(inverse_second, row_height, col_width)
    row_first, frontier = sweep_step(blocks, first_diag, panel_first, structure_first)
    row_second, unused = sweep_step(frontier, second_diag, panel_second, structure_second)
    return (close_packed(row_first), close_packed(row_second))


def solution(mesh):
    in_specs = (
        P(None, None, "row", "col"),
        P(None, None, "row", "col"),
        P("row", None, "col"),
        P(),
        P(None, None, "row", "col"),
        P("row", None, "col"),
        P(),
    )
    out_specs = (P(None, None, "row", "col"), P(None, None, "row", "col"))
    return jax.shard_map(
        on_device, mesh=mesh, in_specs=in_specs, out_specs=out_specs, check_vma=False
    )
```

profile of v0, /device:TPU:0, one launch (start us, length us, event | category | flops | bytes accessed | tf_op | source)
XLA Modules:
  0.0 613.9 jit_solution(9466836030840929645)
XLA Ops:
  7.9 0.7 compare_select_fusion.9
  8.6 29.6 %all-gather.4.cloned.1.call-done = f32[1536,2,128]{2,1,0:T(2,128)} async-done(((f32[192,2,128]{2,1,0:T(2,128)}), f32[1536,2,128]{2,1,0:T(2,128)}) %all-gather.4.cloned.1.call-update) | async-done | bytes 1572880 | tf_op jit(solution)/shard_map/all_gather | solution.py:21
  38.2 10.2 %scatter_custom_fusion.1 = f32[4608,256]{1,0:T(8,128)} fusion(s32[1536]{0:T(1024)S(1)} %compare_select_fusion.9, f32[]{:T(128)} %constant.127.clone.1, f32[192,8,2,128]{3,2,1,0:T(2,128)} %bitcast.143), kind=kCustom, calls=%fused_computation.18 | custom fusion | bytes 6291460 | tf_op jit(solution)/shard_map/scatter | solution.py:24
  48.3 6.8 %reshape_reshape.6 = f32[9,4,128,2,1,128]{5,3,2,1,0,4:T(2,128)} reshape(f32[4608,256]{1,0:T(8,128)} %scatter_custom_fusion.1) | data formatting | bytes 9437184 | tf_op jit(solution)/shard_map/reshape;reshape | solution.py:58
  55.2 5.0 copy.178
  60.1 4.9 all-to-all-start
  65.1 6.8 %reshape.234 = f32[9,512,2,128]{3,2,1,0:T(2,128)} reshape(f32[4608,256]{1,0:T(8,128)} %scatter_custom_fusion.1) | data formatting | bytes 9437184 | tf_op jit(solution)/shard_map/reshape | solution.py:26
  71.9 2.1 constant_dynamic-slice_fusion.4
  74.7 6.2 %scatter_custom_fusion = s32[4608]{0:T(1024)S(1)} fusion(s32[1536]{0:T(1024)S(1)} %compare_select_fusion.9, s32[1536]{0:T(1024)S(1)} %broadcast.296, s32[]{:T(128)} %constant.105.clone.1), kind=kCustom, calls=%fused_computation.102 | custom fusion | bytes 18436 | tf_op jit(solution)/shard_map/scatter | solution.py:61
  81.7 3.5 top_k.40
  85.9 6.2 %copy.183 = f32[9,9,64,128]{2,0,3,1:T(8,128)} copy(f32[9,9,64,128]{3,2,1,0:T(8,128)S(1)} %copy-done) | data formatting | bytes 5308416 | tf_op args[0]
  92.1 8.5 %gather_fusion.3 = f32[432,9,64]{2,1,0:T(8,128)} fusion(f32[9,9,64,128]{2,1,3,0:T(8,128)} %bitcast.129, s32[432]{0:T(512)S(1)} %reshape.261), kind=kCustom, calls=%fused_computation.3 | custom fusion | bytes 1994112 | tf_op jit(solution)/shard_map/vmap(jit(_take))/gather | solution.py:42
  100.5 4.0 copy.184
  104.5 103.6 %all-to-all-done = f32[9,4,128,2,1,128]{5,3,2,0,4,1:T(2,128)} async-done(((f32[9,4,128,2,1,128]{5,3,2,0,4,1:T(2,128)}), f32[9,4,128,2,1,128]{5,3,2,0,4,1:T(2,128)}, u32[]{:S(2)}, u32[]{:S(2)}) %all-to-all-start) | async-done | bytes 4718624 | tf_op jit(solution)/shard_map/all_to_all | solution.py:59
  208.1 8.1 %copy.179 = f32[9,4,128,2,1,128]{2,5,1,3,0,4:T(8,128)} copy(f32[9,4,128,2,1,128]{5,3,2,0,4,1:T(2,128)} %all-to-all-done) | data formatting | bytes 9437184 | tf_op jit(solution)/shard_map/all_to_all | solution.py:59
  216.2 8.3 %copy.181 = f32[9,128,2,512]{3,2,1,0:T(2,128)} copy(f32[9,128,2,512]{1,3,2,0:T(8,128)} %bitcast.128) | data formatting | bytes 9437184 | tf_op jit(solution)/shard_map/reshape | solution.py:60
  224.5 8.3 %gather_fusion.2 = f32[432,2,512]{2,1,0:T(2,128)} fusion(f32[9,128,2,512]{3,2,1,0:T(2,128)} %copy.181, s32[432]{0:T(512)S(1)} %reshape.261), kind=kCustom, calls=%fused_computation.2 | custom fusion | bytes 3542400 | tf_op jit(solution)/shard_map/vmap(jit(_take))/gather | solution.py:42
  232.8 8.3 %fusion.9 = f32[9,2,64,512]{3,2,0,1:T(8,128)} fusion(f32[9,48,9,64]{3,1,0,2:T(8,128)} %bitcast.135, f32[9,48,2,512]{3,2,1,0:T(2,128)} %bitcast.137, pred[9,48]{1,0:T(8,128)(4,1)S(1)} %compare_and_fusion.2), kind=kOutput, calls=%fused_computation.27 | convolution fusion | flops 3058338816 | bytes 5124528 | tf_op jit(solution)/shard_map/ijak,jknw->inaw/dot_general | solution.py:67
  241.1 10.4 %all_gather.14 = f32[1536,1,128]{2,1,0:T(1,128)S(1)} all-gather(f32[192,1,128]{2,1,0:T(1,128)S(1)} %copy-done.5), channel_id=1, replica_groups=mesh['row'=8,'col'=4] {'row'}, dimensions={0}, use_global_device_ids=true | all-gather | bytes 884736 | tf_op jit(solution)/shard_map/all_gather | solution.py:21
  251.4 6.0 scatter_custom_fusion.3
  257.5 3.8 copy.205
  261.2 4.6 all-to-all-start.1
  266.1 0.8 constant_dynamic-slice_fusion.5
  267.1 3.5 top_k.37
  271.3 3.6 gather_fusion
  274.9 4.2 gather_fusion.1
  279.2 7.3 %convolution_bitcast_fusion = f32[2,9,512,128]{2,3,0,1:T(8,128)} fusion(f32[9,24,9,128]{3,1,0,2:T(8,128)} %bitcast.136, f32[9,24,2,512]{3,2,1,0:T(2,128)S(1)} %bitcast.133, pred[9,24]{1,0:T(8,128)(4,1)S(1)} %compare_and_fusion.3), kind=kOutput, calls=%fused_computation.20 | convolution fusion | flops 3058117632 | bytes 6598872 | tf_op jit(solution)/shard_map/iakw,ijab->kjwb/dot_general | solution.py:72
  286.4 8.2 %copy.173 = f32[2,9,512,128]{3,0,1,2:T(2,128)} copy(f32[2,9,512,128]{2,3,0,1:T(8,128)} %convolution_bitcast_fusion) | data formatting | bytes 9437184 | tf_op jit(solution)/shard_map/iakw,ijab->kjwb/transpose | solution.py:72
  294.6 14.9 %reduce-scatter.4.cloned.1.call-done = f32[9,2,64,128]{3,2,0,1:T(8,128)} async-done(((f32[9,2,64,512]{3,2,0,1:T(8,128)}), f32[9,2,64,128]{3,2,0,1:T(8,128)}) %reduce-scatter.4.cloned.1.call-update) | async-done | bytes 589840 | tf_op jit(solution)/shard_map/reduce_scatter | solution.py:70
  309.5 2.3 copy.185
  311.9 3.6 gather_fusion.4
  315.4 3.2 convolution_bitcast_fusion.2
  318.6 2.3 copy.187
  321.0 1.8 constant_dynamic-slice_fusion.1
  322.8 6.8 %scatter_custom_fusion.2 = s32[5632]{0:T(1024)S(1)} fusion(s32[1536]{0:T(1024)} %copy-done.10, s32[1536]{0:T(1024)} %copy-done.9, s32[]{:T(128)} %constant.105.clone.1), kind=kCustom, calls=%fused_computation.98 | custom fusion | bytes 23040 | tf_op jit(solution)/shard_map/scatter | solution.py:61
  329.7 3.8 copy.193
  333.7 4.2 top_k.50
  339.8 8.3 %all-to-all-done.1 = f32[11,4,128,1,1,128]{5,2,0,4,3,1:T(8,128)} async-done(((f32[11,4,128,1,1,128]{5,2,0,4,3,1:T(8,128)}), f32[11,4,128,1,1,128]{5,2,0,4,3,1:T(8,128)}, u32[]{:S(2)}, u32[]{:S(2)}) %all-to-all-start.1) | async-done | bytes 2883616 | tf_op jit(solution)/shard_map/all_to_all | solution.py:59
  348.0 5.3 copy.206
  353.3 3.1 reshape.293
  356.5 10.8 %gather_fusion.7 = f32[528,512]{1,0:T(8,128)} fusion(f32[11,128,512]{2,1,0:T(8,128)S(1)} %reshape.293, s32[528]{0:T(1024)S(1)} %reshape.295), kind=kCustom, calls=%fused_computation.7 | custom fusion | bytes 2166912 | tf_op jit(solution)/shard_map/vmap(jit(_take))/gather | solution.py:42
  367.8 51.5 %all-reduce.9.cloned.1.call-done = (f32[2,2,512,128]{3,1,0,2:T(2,128)}, f32[2,9,512,128]{3,0,1,2:T(2,128)}) async-done(((f32[2,2,512,128]{3,1,0,2:T(2,128)}, f32[2,9,512,128]{3,0,1,2:T(2,128)}), (f32[2,2,512,128]{3,1,0,2:T(2,128)}, f32[2,9,512,128]{3,0,1,2:T(2,128)})) %all-reduce.9.cloned.1.call-update) | async-done | bytes 5767184
  419.3 0.9 constant_dynamic-slice_fusion.6
  420.2 1.1 constant_dynamic-slice_fusion.7
  421.5 0.8 copy-done.2
  422.8 5.5 fusion.79
  428.3 9.7 %copy.208 = f32[11,11,64,128]{2,1,3,0:T(8,128)} copy(f32[11,11,64,128]{3,0,2,1:T(8,128)} %fusion.79) | data formatting | bytes 7929856 | tf_op jit(solution)/shard_map/vmap(jit(_take))/transpose | solution.py:42
  438.0 11.8 %gather_fusion.8 = f32[528,11,64]{2,1,0:T(8,128)} fusion(f32[11,11,64,128]{2,1,3,0:T(8,128)} %copy.208, s32[528]{0:T(1024)S(1)} %reshape.295), kind=kCustom, calls=%fused_computation.8 | custom fusion | bytes 2977920 | tf_op jit(solution)/shard_map/vmap(jit(_take))/gather | solution.py:42
  449.8 3.3 copy.209
  453.1 7.2 %fusion.19 = f32[11,1,64,512]{3,2,0,1:T(8,128)} fusion(f32[11,48,11,64]{3,1,0,2:T(8,128)S(1)} %bitcast.127, pred[11,48]{1,0:T(8,128)(4,1)S(1)} %compare_and_fusion.1, f32[11,48,512]{2,1,0:T(8,128)S(1)} %bitcast.140), kind=kOutput, calls=%fused_computation.34 | convolution fusion | flops 2284440576 | bytes 4010512 | tf_op jit(solution)/shard_map/ijak,jknw->inaw/dot_general | solution.py:67
  460.7 4.4 top_k.43
  465.7 9.7 %gather_fusion.6 = f32[264,512]{1,0:T(8,128)S(1)} fusion(f32[11,64,512]{2,1,0:T(8,128)} %bitcast.132, s32[264]{0:T(512)S(1)} %reshape.279), kind=kCustom, calls=%fused_computation.6 | custom fusion | bytes 1083456 | tf_op jit(solution)/shard_map/vmap(jit(_take))/gather | solution.py:42
  475.4 5.5 pad_maximum_fusion
  480.9 7.0 %gather_fusion.5 = f32[264,11,128]{2,1,0:T(8,128)} fusion(f32[11,11,64,128]{3,1,2,0:T(8,128)} %pad_maximum_fusion, s32[264]{0:T(512)S(1)} %reshape.279), kind=kCustom, calls=%fused_computation.5 | custom fusion | bytes 2975808 | tf_op jit(solution)/shard_map/vmap(jit(_take))/gather | solution.py:42
  487.9 7.1 %convolution_bitcast_fusion.1 = f32[1,11,512,128]{2,3,1,0:T(8,128)S(1)} fusion(f32[11,24,11,128]{3,2,1,0:T(8,128)} %bitcast.141, pred[11,24]{1,0:T(8,128)(4,1)S(1)} %copy.192, f32[11,24,512]{2,1,0:T(8,128)S(1)} %bitcast.138), kind=kOutput, calls=%fused_computation.24 | convolution fusion | flops 2284305408 | bytes 4911368 | tf_op jit(solution)/shard_map/iakw,ijab->kjwb/dot_general | solution.py:72
  495.0 5.3 copy.200
  500.4 4.1 gather_fusion.9
  504.6 0.8 convolution_bitcast_fusion.3
  505.4 0.8 copy.210
  506.3 61.2 %all-reduce.7.cloned.1.call-done = f32[1,11,512,128]{3,0,1,2:T(1,128)} async-done(((f32[1,11,512,128]{3,0,1,2:T(1,128)}), f32[1,11,512,128]{3,0,1,2:T(1,128)}) %all-reduce.7.cloned.1.call-update) | async-done | bytes 2883600
  567.5 1.3 dynamic-slice_negate_fusion
  568.8 35.9 %reduce-scatter.8.cloned.1.call-done = f32[1,1,64,128]{3,1,0,2:T(1,128)} async-done(((f32[1,1,512,128]{3,1,0,2:T(1,128)}), f32[1,1,64,128]{3,1,0,2:T(1,128)}) %reduce-scatter.8.cloned.1.call-update) | async-done | bytes 32784 | tf_op jit(solution)/shard_map/reduce_scatter | solution.py:80
  604.7 0.8 add.205
  605.8 0.8 copy.213
  (114 shorter events, 8.0 us)
Async XLA Ops:
  7.2 31.0 %all-gather.4.cloned.1.call-start = ((), (), s32[]{:S(2)}) async-start(), calls=%async_computation.5 | async-start | bytes 1769472 | tf_op jit(solution)/shard_map/all_gather | solution.py:21
  60.1 148.0 %all-to-all-start = ((f32[9,4,128,2,1,128]{5,3,2,0,4,1:T(2,128)}), f32[9,4,128,2,1,128]{5,3,2,0,4,1:T(2,128)}, u32[]{:S(2)}, u32[]{:S(2)}) async-start(f32[9,4,128,2,1,128]{5,3,2,0,4,1:T(2,128)} %copy.178), calls=%async_computation | async-start | bytes 9437184 | tf_op jit(solution)/shard_map/all_to_all | solution.py:59
  65.1 209.9 %all-gather.6.cloned.1.call-start = ((), (), s32[]{:S(2)}) async-start(), calls=%async_computation.6 | async-start | bytes 2949120 | tf_op jit(solution)/shard_map/all_gather | solution.py:57
  71.9 13.9 %copy-start = (f32[9,9,64,128]{3,2,1,0:T(8,128)S(1)}, f32[9,9,64,128]{3,2,1,0:T(8,128)}, u32[]{:S(2)}) copy-start(f32[9,9,64,128]{3,2,1,0:T(8,128)} %param.7) | copy-start | bytes 7962628
  74.0 235.5 %reduce-scatter.4.cloned.1.call-start = ((), (), s32[]{:S(2)}) async-start(), calls=%async_computation.7 | async-start | bytes 2949120 | tf_op jit(solution)/shard_map/reduce_scatter | solution.py:70
  74.1 0.6 copy-start.9
  80.9 0.6 copy-start.6
  232.8 8.3 %copy-start.5 = (f32[192,1,128]{2,1,0:T(1,128)S(1)}, f32[192,1,128]{2,1,0:T(1,128)}, u32[]{:S(2)}) copy-start(f32[192,1,128]{2,1,0:T(1,128)} %param.12) | copy-start | bytes 294916
  241.0 10.4 %copy-start.8 = (s32[1536]{0:T(1024)S(1)}, s32[1536]{0:T(1024)}, u32[]{:S(2)}) copy-start(s32[1536]{0:T(1024)} %param.13) | copy-start | bytes 18436
  251.4 9.8 %copy-start.10 = (s32[1536]{0:T(1024)}, s32[1536]{0:T(1024)S(1)}, u32[]{:S(2)}) copy-start(s32[1536]{0:T(1024)S(1)} %compare_select_fusion.4) | copy-start | bytes 18436
  261.2 86.8 %all-to-all-start.1 = ((f32[11,4,128,1,1,128]{5,2,0,4,3,1:T(8,128)}), f32[11,4,128,1,1,128]{5,2,0,4,3,1:T(8,128)}, u32[]{:S(2)}, u32[]{:S(2)}) async-start(f32[11,4,128,1,1,128]{5,2,0,4,3,1:T(8,128)} %copy.205), calls=%async_computation.2 | async-start | bytes 5767168 | tf_op jit(solution)/shard_map/all_to_all | solution.py:59
  265.8 153.5 %all-reduce.9.cloned.1.call-start = ((), (), s32[]{:S(2)}) async-start(), calls=%async_computation.12 | async-start | bytes 11534336
  270.8 4.1 copy-start.11
  321.0 144.8 %all-gather.8.cloned.1.call-start = ((), (), s32[]{:S(2)}) async-start(), calls=%async_computation.8 | async-start | bytes 1802240 | tf_op jit(solution)/shard_map/all_gather | solution.py:57
  322.8 177.7 %reduce-scatter.6.cloned.1.call-start = ((), (), s32[]{:S(2)}) async-start(), calls=%async_computation.9 | async-start | bytes 1802240 | tf_op jit(solution)/shard_map/reduce_scatter | solution.py:70
  329.7 8.8 %copy-start.13 = (u32[32]{0:T(128)S(1)}, u32[32]{0:T(128)}, u32[]{:S(2)}) copy-start(u32[32]{0:T(128)} %constant.288) | copy-start | bytes 388
  356.5 10.8 %copy-start.3 = (f32[9,2,64,128]{3,2,0,1:T(8,128)S(1)}, f32[9,2,64,128]{3,2,0,1:T(8,128)}, u32[]{:S(2)}) copy-start(f32[9,2,64,128]{3,2,0,1:T(8,128)} %reduce-scatter.4.cloned.1.call-done) | copy-start | bytes 1769476
  367.3 54.1 %copy-start.4 = (f32[2,2,64,128]{3,2,1,0:T(8,128)S(1)}, f32[2,2,64,128]{3,2,1,0:T(8,128)}, u32[]{:S(2)}) copy-start(f32[2,2,64,128]{3,2,1,0:T(8,128)} %param.8) | copy-start | bytes 393220
  421.5 0.9 copy-start.2
  449.8 3.3 copy-start.1
  453.1 12.2 %copy-start.12 = (s32[4]{0:T(128)S(1)}, s32[4]{0:T(128)}, u32[]{:S(2)}) copy-start(s32[4]{0:T(128)} %copy-done.11) | copy-start | bytes 52
  460.4 107.1 %all-reduce.7.cloned.1.call-start = ((), (), s32[]{:S(2)}) async-start(), calls=%async_computation.11 | async-start | bytes 5767168
  500.3 104.4 %copy-start.7 = (f32[1,1,64,128]{3,2,1,0:T(8,128)S(1)}, f32[1,1,64,128]{3,2,1,0:T(8,128)}, u32[]{:S(2)}) copy-start(f32[1,1,64,128]{3,2,1,0:T(8,128)} %param.11) | copy-start | bytes 98308
  500.4 104.3 %reduce-scatter.8.cloned.1.call-start = ((), (), s32[]{:S(2)}) async-start(), calls=%async_computation.10 | async-start | bytes 294912 | tf_op jit(solution)/shard_map/reduce_scatter | solution.py:80
Sparse Core Ops, SparseCore 0:
  9.9 28.2 all-gather.3
  74.2 108.2 all-gather.5
  241.2 68.2 reduce-scatter.3
  321.1 98.1 all-reduce.8
  421.3 35.6 all-gather.7
  460.5 33.5 reduce-scatter.5
  500.5 66.9 all-reduce.6
  571.1 33.5 reduce-scatter.7
where the time goes:
time: 624 us; the launch traced here: 614 us
  waiting for transfers between devices  306 us (49%)
  local copies, waits for them, and re-layouts  208 us (33%)
  matrix products  33.9 us (5%)
  other arithmetic  30.4 us (5%)
  between operations  15.7 us (3%)
  blocking collectives  10.4 us (2%)
  starting transfers between devices  10.1 us (2%)
    unnamed x10, waiting for transfers between devices  114 us
    all_to_all x2, waiting for transfers between devices, sweep_step(): lax.all_to_all(regrouped, 'col', split_axis=1, concat_axis=4, tiled=True)  112 us
    gather x17, local copies, waits for them, and re-layouts, take_along(): jnp.take(portion, picked, axis=take_axis)  79.2 us
    reduce_scatter x1, waiting for transfers between devices, sweep_step(): lax.psum_scatter(diag_terms, 'row', scatter_dimension=2, tiled=True)  35.9 us
    all_gather x1, waiting for transfers between devices, expand_panel(): gathered = lax.all_gather(panel_part, 'row', axis=0, tiled=True)  29.6 us
    scatter x2, local copies, waits for them, and re-layouts, expand_panel(): jnp.zeros((tile_count * TILE, flattened.shape[1]), jnp.float32)  16.2 us
    top_k x4, other arithmetic, pick_slots(): chosen = lax.top_k(ranking, CAP)[1]  15.6 us
    another operation x3, local copies, waits for them, and re-layouts, sweep_step(): spread.reshape(tile_count, TILE // col_width, col_width, new_tiles, 1, co...  15.5 us
  transfers between devices with their start and end apart: 10, of which 7 were waited for; matrix products, arithmetic and copies ran while one was open for 40% of the time, Pallas kernels for 0%

commit v1 on v0

v1 whole, which is shorter than its diff:
```python
import jax
import jax.numpy as jnp
from jax import lax
from jax.sharding import PartitionSpec as P

TILE = 512
GRAIN = 16
CAP = 6


def open_packed(packed, row_height, col_width):
    return packed.reshape(packed.shape[0], packed.shape[1], row_height, col_width)


def close_packed(tiles):
    depth = tiles.shape[2] * tiles.shape[3] // 128
    return tiles.reshape(tiles.shape[0], tiles.shape[1], depth, 128)


def product(left, right, left_dim=1):
    return lax.dot_general(
        left,
        right,
        (((left_dim,), (0,)), ((), ())),
        precision=lax.Precision.HIGH,
        preferred_element_type=jnp.float32,
    )


def entry_ranks(structure):
    group = structure // GRAIN
    order = jnp.arange(structure.shape[0], dtype=jnp.int32)
    same = (group[:, None] == group[None, :]) & (order[None, :] < order[:, None])
    return jnp.sum(same.astype(jnp.int32), axis=1)


def slots_within(structure, ranks, height):
    owner = structure % TILE // height
    group = structure // TILE * (height // GRAIN) + structure % height // GRAIN
    return owner, group * CAP + ranks


def one_hot(marks, count):
    return (jnp.arange(count, dtype=jnp.int32)[:, None] == marks[None, :]).astype(jnp.float32)


def local_rows(structure, marks, count, height):
    row = structure // TILE * height + structure % height
    match = jnp.arange(count, dtype=jnp.int32)[:, None] == marks[None, :]
    return jnp.max(jnp.where(match, row[None, :], -1), axis=1)


def on_device(
    ancestor,
    inverse_first,
    panel_first,
    structure_first,
    inverse_second,
    panel_second,
    structure_second,
):
    rows = lax.axis_size("row")
    cols = lax.axis_size("col")
    height = TILE // rows
    width = TILE // cols
    halves = width // height
    row_index = lax.axis_index("row")
    col_index = lax.axis_index("col")
    blocks = open_packed(ancestor, height, width)
    first_diag = open_packed(inverse_first, height, width)
    second_diag = open_packed(inverse_second, height, width)
    tiles = blocks.shape[0]
    first = first_diag.shape[0]
    second = second_diag.shape[0]
    every = first + second
    limit = tiles * TILE
    first_width = first * width

    panels = jnp.concatenate(
        [panel_first.reshape(-1, first_width), panel_second.reshape(-1, second * width)], axis=1
    )
    both = lax.all_gather(panels, "row", axis=0, tiled=True)
    whole_first = both[:, :first_width]
    whole_second = both[:, first_width:]

    above = structure_second < limit
    ranks_first = entry_ranks(structure_first)
    ranks_second = entry_ranks(structure_second)
    row_slots = tiles * height // GRAIN * CAP
    col_slots = tiles * width // GRAIN * CAP
    low_slots = first * TILE // GRAIN * CAP
    owner, slot = slots_within(structure_first, ranks_first, height)
    row_marks_first = jnp.where(owner == row_index, slot, -1)
    owner, slot = slots_within(structure_second, ranks_second, height)
    row_marks_second = jnp.where(above & (owner == row_index), slot, -1)
    owner, slot = slots_within(structure_first, ranks_first, width)
    all_marks_first = owner * col_slots + slot
    col_marks_first = jnp.where(owner == col_index, slot, -1)
    owner, slot = slots_within(structure_second, ranks_second, width)
    all_marks_second = jnp.where(above, owner * col_slots + slot, -1)
    col_marks_second = jnp.where(above & (owner == col_index), slot, -1)
    below = structure_second - limit
    low_marks = jnp.where(above, -1, below // GRAIN * CAP + ranks_second)
    low_match = jnp.arange(low_slots, dtype=jnp.int32)[:, None] == low_marks[None, :]
    low_rows = jnp.max(jnp.where(low_match, below[None, :], -1), axis=1)

    take_first = one_hot(row_marks_first, row_slots)
    take_second = one_hot(
        jnp.where(above, row_marks_second, row_slots + low_marks), row_slots + low_slots
    )
    part_first = product(take_first, whole_first)
    part_second = product(take_second, whole_second)
    part_first = part_first.reshape(row_slots, first, halves, height).transpose(0, 2, 1, 3)
    part_first = part_first.reshape(row_slots * first, width)
    part_second = part_second.reshape(row_slots + low_slots, second, halves, height)
    part_second = part_second.transpose(0, 2, 1, 3)
    part_second = part_second.reshape((row_slots + low_slots) * second, width)
    spread = lax.all_gather(jnp.concatenate([part_first, part_second], axis=0), "col", axis=0)
    cut = part_first.shape[0]
    got_first = spread[:, :cut].reshape(cols, row_slots, halves, first, height)
    got_second = spread[:, cut:].reshape(cols, row_slots + low_slots, halves, second, height)
    got_first = got_first.transpose(1, 0, 2, 3, 4).reshape(row_slots, rows, first * height)
    got_second = got_second.transpose(1, 0, 2, 3, 4).reshape(-1, rows, second * height)
    upper_second = got_second[:row_slots]
    low_second = got_second[row_slots:].reshape(low_slots, second * TILE)

    flat = blocks.transpose(0, 2, 1, 3).reshape(tiles * height, tiles * width)
    kept_rows = jnp.concatenate(
        [
            local_rows(structure_first, row_marks_first, row_slots, height),
            local_rows(structure_second, row_marks_second, row_slots, height),
        ]
    )
    take_kept = (
        kept_rows[:, None] == jnp.arange(tiles * height, dtype=jnp.int32)[None, :]
    ).astype(jnp.float32)
    kept = product(take_kept, flat)

    place = jnp.arange(first * TILE, dtype=jnp.int32)
    place_row = place // (first * height)
    place_tile = place // height % first
    named = place_tile * TILE + place_row * height + place % height
    meet_low = (named[:, None] == low_rows[None, :]).astype(jnp.float32)
    first_at_low = product(got_first.reshape(row_slots, first * TILE), meet_low)
    folded = product(first_at_low, low_second).reshape(row_slots, rows, second * height)
    left = jnp.concatenate(
        [
            jnp.concatenate([got_first, -folded], axis=2),
            jnp.concatenate(
                [jnp.zeros((row_slots, rows, first * height), jnp.float32), upper_second], axis=2
            ),
        ],
        axis=0,
    )
    partial = product(left.reshape(2 * row_slots, every * TILE), kept, 0)
    partial = partial.reshape(rows, every * height, tiles * width)

    own_low = jnp.arange(first * height, dtype=jnp.int32)
    own_low = own_low // height * TILE + row_index * height + own_low % height
    own_meet = (own_low[:, None] == low_rows[None, :]).astype(jnp.float32)
    own_second = product(own_meet, low_second)
    flat_diag = first_diag.transpose(0, 2, 1, 3).reshape(first * height, first_width)
    low_partial = product(own_second, flat_diag, 0)
    low_partial = low_partial.reshape(rows, second * height, first_width)

    slabs = [low_partial[:, :, k * width : (k + 1) * width] for k in range(first)]
    slabs.append(jnp.zeros((rows, (every - first * second) * height, width), jnp.float32))
    joined = jnp.concatenate([partial, jnp.concatenate(slabs, axis=1)], axis=2)
    summed = lax.psum_scatter(joined, "row", scatter_dimension=0, tiled=False)
    image = summed[:, : tiles * width]
    step = second * height
    low_image = jnp.concatenate(
        [summed[k * step : (k + 1) * step, tiles * width :] for k in range(first)], axis=1
    )

    edge = first * height
    column_ids = jnp.arange(tiles * width, dtype=jnp.int32)
    col_rows_first = local_rows(structure_first, col_marks_first, col_slots, width)
    col_rows_second = local_rows(structure_second, col_marks_second, col_slots, width)
    pick_first = (column_ids[:, None] == col_rows_first[None, :]).astype(jnp.float32)
    pick_second = (column_ids[:, None] == col_rows_second[None, :]).astype(jnp.float32)
    picked = jnp.concatenate([product(image, pick_first), product(image[edge:], pick_second)], axis=0)
    met = lax.all_gather(picked, "col", axis=0)
    met = met.transpose(1, 0, 2).reshape(-1, cols * col_slots)
    dense_first = product(one_hot(all_marks_first, cols * col_slots), whole_first)
    dense_second = product(one_hot(all_marks_second, cols * col_slots), whole_second)
    corner = product(met[: every * height], dense_first)
    low_block = low_image - corner[edge:]
    low_all = lax.all_gather(low_block, "col", axis=0)
    low_all = low_all.transpose(1, 0, 2).reshape(second * height, first * TILE)
    spot = jnp.arange(first * TILE, dtype=jnp.int32)
    spot = spot // width % first * TILE + spot // first_width * width + spot % width
    below_marks = jnp.where(above, -1, below)
    dense_low = product(
        (spot[:, None] == below_marks[None, :]).astype(jnp.float32), whole_second
    )
    final = product(met[every * height :], dense_second) + product(low_all, dense_low)

    def tiled(matrix, up, across):
        return matrix.reshape(up, height, across, width).transpose(0, 2, 1, 3)

    row_first = jnp.concatenate(
        [-tiled(image[:edge], first, tiles), first_diag + tiled(corner[:edge], first, first)], axis=1
    )
    row_second = jnp.concatenate(
        [
            -tiled(image[edge:], second, tiles),
            -tiled(low_block, second, first),
            second_diag + tiled(final, second, second),
        ],
        axis=1,
    )
    return (close_packed(row_first), close_packed(row_second))


def solution(mesh):
    in_specs = (
        P(None, None, "row", "col"),
        P(None, None, "row", "col"),
        P("row", None, "col"),
        P(),
        P(None, None, "row", "col"),
        P("row", None, "col"),
        P(),
    )
    out_specs = (P(None, None, "row", "col"), P(None, None, "row", "col"))
    return jax.shard_map(
        on_device, mesh=mesh, in_specs=in_specs, out_specs=out_specs, check_vma=False
    )
```

time: 624 us -> 280 us (0.45)
  local copies, waits for them, and re-layouts: 208 us -> 27.7 us
  waiting for transfers between devices: 306 us -> 164 us
  other arithmetic: 30.4 us -> 18.6 us
  starting transfers between devices: 10.1 us -> 0.63 us
    unnamed x10 -> x4, waiting for transfers between devices: 114 us -> 0.07 us
    all_to_all x2 -> x0, waiting for transfers between devices: 112 us -> none  [sweep_step(): lax.all_to_all(regrouped, 'col', split_axis=1, concat_axis=4, tiled=True)]
    gather x17 -> x0, local copies, waits for them, and re-layouts: 79.2 us -> none  [take_along(): jnp.take(portion, picked, axis=take_axis)]
    all_gather x3, waiting for transfers between devices: 29.6 us -> 96.3 us  [the longest x1 39.3 us: on_device(): lax.all_gather(jnp.concatenate([part_first, part_second], axis=0), 'col',...]
    scatter x4 -> x0, local copies, waits for them, and re-layouts: 29.1 us -> none  [the longest x2 16.2 us: expand_panel(): jnp.zeros((tile_count * TILE, flattened.shape[1]), jnp.float32)]
    transpose x5 -> x4, local copies, waits for them, and re-layouts: 26.3 us -> 5.2 us  [the longest x1 3.14 us: on_device(): got_first.transpose(1, 0, 2, 3, 4).reshape(row_slots, rows, first * height)]
    reduce_scatter x3 -> x1, waiting for transfers between devices: 50.8 us -> 67.3 us  [on_device(): summed = lax.psum_scatter(joined, 'row', scatter_dimension=0, tiled=False)]
    reshape x17 -> x4, local copies, waits for them, and re-layouts: 19.1 us -> 2.66 us  [the longest x1 2.23 us: on_device(): got_first = spread[:, :cut].reshape(cols, row_slots, halves, first, height)]
  transfers between devices with their start and end apart: 10 -> 4, of which waited for: 7 -> 4; matrix products, arithmetic and copies ran while one was open for 40% -> 10% of each run, Pallas kernels for 0% -> 0%
where the time goes in v1:
time: 280 us; the launch traced here: 275 us
  waiting for transfers between devices  164 us (59%)
  matrix products  35.5 us (13%)
  local copies, waits for them, and re-layouts  27.7 us (10%)
  other arithmetic  18.6 us (7%)
  between operations  14.5 us (5%)
  blocking collectives  14.1 us (5%)
    reduce_scatter x1, waiting for transfers between devices, on_device(): summed = lax.psum_scatter(joined, 'row', scatter_dimension=0, tiled=False)  67.3 us
    all_gather x1, waiting for transfers between devices, on_device(): lax.all_gather(jnp.concatenate([part_first, part_second], axis=0), 'col',...  39.3 us
    dot_general x16, matrix products, product(): lax.dot_general(left, right, (((left_dim,), (0,)), ((), ())), precision=l...  35.5 us
    all_gather x1, waiting for transfers between devices, on_device(): met = lax.all_gather(picked, 'col', axis=0)  33 us
    all_gather x1, waiting for transfers between devices, on_device(): both = lax.all_gather(panels, 'row', axis=0, tiled=True)  23.9 us
    all_gather x1, blocking collectives, on_device(): low_all = lax.all_gather(low_block, 'col', axis=0)  14.1 us
  transfers between devices with their start and end apart: 4, of which 4 were waited for; matrix products, arithmetic and copies ran while one was open for 10% of the time, Pallas kernels for 0%

profile of v1, /device:TPU:0, one launch (start us, length us, event | category | flops | bytes accessed | tf_op | source)
XLA Modules:
  0.0 274.7 jit_solution(11923540824336374075)
XLA Ops:
  7.2 0.9 copy.54
  8.2 1.6 pad_maximum_fusion.4
  9.9 0.7 add_select_fusion.13
  10.6 0.7 add_select_fusion.7
  11.3 2.7 convert_reduce_fusion
  13.9 0.7 add_select_fusion.19
  14.7 2.7 convert_reduce_fusion.1
  17.3 0.8 multiply_add_fusion
  18.1 23.9 %all-gather.7.cloned.1.call-done = f32[1536,384]{1,0:T(8,128)} async-done(((f32[192,384]{1,0:T(8,128)}), f32[1536,384]{1,0:T(8,128)}) %all-gather.7.cloned.1.call-update) | async-done | bytes 2359312 | tf_op jit(solution)/shard_map/all_gather | solution.py:82
  42.1 2.4 fusion.28
  44.5 0.3 copy.29
  44.8 0.3 reshape.188
  45.1 2.4 fusion.8
  47.5 0.8 pad_maximum_fusion.1
  48.3 0.3 reduce-scatter.2.cloned.1.call-start
  48.9 1.7 copy.33
  50.6 1.0 pad.13.clone
  51.7 0.3 select_reduce_fusion.4
  51.9 0.3 select_reduce_fusion.3
  52.3 0.4 select_reduce_fusion.2
  52.7 2.4 convolution_bitcast_fusion
  55.1 39.3 %all-gather.9.cloned.1.call-done = f32[4128,128]{1,0:T(8,128)} async-done(((f32[1032,128]{1,0:T(8,128)}), f32[4128,128]{1,0:T(8,128)}) %all-gather.9.cloned.1.call-update) | async-done | bytes 2113552 | tf_op jit(solution)/shard_map/all_gather | solution.py:118
  94.4 2.4 slice.87
  96.8 1.7 copy.42
  98.5 0.3 slice.88
  98.8 0.9 slice.89
  99.6 1.2 slice.86
  100.9 0.5 fusion.46
  101.3 0.4 fusion.133
  101.7 0.7 fusion.132
  102.4 2.2 reshape.189
  104.7 3.1 %copy.30 = f32[216,4,2,2,64]{0,4,3,2,1:T(8,128)S(1)} copy(f32[216,4,2,2,64]{4,3,2,0,1:T(2,128)} %bitcast.81) | data formatting | bytes 1769472 | tf_op jit(solution)/shard_map/transpose | solution.py:122
  107.8 1.0 fusion.30
  108.8 1.7 convolution_negate_fusion
  110.6 6.3 %fusion.10 = f32[8,192,1152]{2,1,0:T(8,128)S(1)} fusion(f32[432,1152,1]{1,0,2:T(8,128)S(1)} %convolution_bitcast_fusion, f32[216,8,64]{0,2,1:T(8,128)S(1)} %bitcast.88, f32[216,8,64]{0,2,1:T(8,128)S(1)} %convolution_negate_fusion, f32[216,8,128]{0,2,1:T(8,128)S(1)} %bitcast.76), kind=kOutput, calls=%fused_computation.18 | convolution fusion | flops 4589125632 | bytes 10838016 | tf_op jit(solution)/shard_map/dot_general | solution.py:21
  116.9 3.9 %maximum_maximum_fusion = f32[8,192,1280]{2,1,0:T(8,128)} fusion(f32[8,64,128]{2,1,0:T(8,128)S(1)} %copy-done.6, f32[8,64,128]{2,1,0:T(8,128)S(1)} %get-tuple-element.18, f32[8,192,1152]{2,1,0:T(8,128)S(1)} %fusion.10, f32[192,1280]{1,0:T(8,128)S(1)} %copy-done.2), kind=kLoop, calls=%fused_computation.9 | loop fusion | flops 5898240 | bytes 16449536 | tf_op jit(solution)/shard_map/concatenate | solution.py:168
  120.8 0.2 all-gather.11.cloned.1.call-start
  121.1 0.4 select_reduce_fusion
  121.5 0.4 select_reduce_fusion.1
  121.9 67.3 %reduce-scatter.2.cloned.1.call-done = f32[1,192,1280]{2,1,0:T(8,128)} async-done(((f32[8,192,1280]{2,1,0:T(8,128)}), f32[1,192,1280]{2,1,0:T(8,128)}) %reduce-scatter.2.cloned.1.call-update) | async-done | bytes 983056 | tf_op jit(solution)/shard_map/reduce_scatter | solution.py:169
  189.2 1.7 fusion.21
  190.9 2.0 fusion.20
  193.0 0.8 pad_maximum_fusion.2
  193.8 2.6 fusion.4
  196.5 3.9 %fusion.1 = f32[1728,128]{1,0:T(8,128)} fusion(s32[1536]{0:T(1024)S(1)} %get-tuple-element.8, f32[1536,384]{1,0:T(8,128)S(1)} %copy-done.7), kind=kOutput, calls=%fused_computation.3 | convolution fusion | flops 2041085952 | bytes 1679360 | tf_op jit(solution)/shard_map/dot_general | solution.py:21
  200.3 4.3 %fusion = f32[1728,256]{1,0:T(8,128)} fusion(s32[1536]{0:T(1024)S(1)} %get-tuple-element.11, f32[1536,384]{1,0:T(8,128)S(1)} %copy-done.7), kind=kOutput, calls=%fused_computation.2 | convolution fusion | flops 4079517696 | bytes 3350528 | tf_op jit(solution)/shard_map/dot_general | solution.py:21
  204.6 1.1 neg.32
  205.8 0.8 fusion.131
  206.6 33.0 %all-gather.11.cloned.1.call-done = f32[1024,432]{1,0:T(8,128)} async-done(((f32[256,432]{1,0:T(8,128)}), f32[1024,432]{1,0:T(8,128)}) %all-gather.11.cloned.1.call-update) | async-done | bytes 1769488 | tf_op jit(solution)/shard_map/all_gather | solution.py:183
  239.6 3.1 %copy.53 = f32[4,256,432]{2,0,1:T(4,128)S(1)} copy(f32[4,256,432]{2,1,0:T(8,128)} %bitcast.89) | data formatting | bytes 3538944 | tf_op jit(solution)/shard_map/all_gather | solution.py:183
  242.8 0.3 slice.95
  243.1 0.8 slice.100
  243.9 1.3 slice.77
  245.3 2.3 fusion.134
  247.7 0.1 bitcast_add_fusion
  247.9 0.4 copy-done.10
  248.4 1.1 copy.39
  249.5 0.9 fusion.126
  250.4 14.1 %all-gather.2 = f32[256,256]{1,0:T(8,128)S(1)} all-gather(f32[64,256]{1,0:T(8,128)S(1)} %get-tuple-element.7), channel_id=4, replica_groups=mesh['row'=8,'col'=4] {'col'}, dimensions={0}, use_global_device_ids=true | all-gather | bytes 327680 | tf_op jit(solution)/shard_map/all_gather | solution.py:189
  264.5 0.2 copy.37
  264.7 0.4 slice.83
  265.2 1.3 fusion.135
  266.5 0.4 fusion.36
  267.0 0.9 copy.40
  (52 shorter events, 1.1 us)
Async XLA Ops:
  7.2 34.9 %all-gather.7.cloned.1.call-start = ((), (), s32[]{:S(2)}) async-start(), calls=%async_computation.1 | async-start | bytes 2654208 | tf_op jit(solution)/shard_map/all_gather | solution.py:82
  9.8 84.6 %all-gather.9.cloned.1.call-start = ((), (), s32[]{:S(2)}) async-start(), calls=%async_computation.3 | async-start | bytes 2641920 | tf_op jit(solution)/shard_map/all_gather | solution.py:118
  44.5 4.2 %copy-start.11 = (f32[2,2,64,128]{3,2,1,0:T(8,128)S(1)}, f32[2,2,64,128]{3,2,1,0:T(8,128)}, u32[]{:S(2)}) copy-start(f32[2,2,64,128]{3,2,1,0:T(8,128)} %param.8) | copy-start | bytes 393220
  44.8 4.1 %copy-start.3 = (f32[9,9,64,128]{3,2,1,0:T(8,128)S(1)}, f32[9,9,64,128]{3,2,1,0:T(8,128)}, u32[]{:S(2)}) copy-start(f32[9,9,64,128]{3,2,1,0:T(8,128)} %param.7) | copy-start | bytes 7962628
  48.3 140.9 %reduce-scatter.2.cloned.1.call-start = ((), (), s32[]{:S(2)}) async-start(), calls=%async_computation.2 | async-start | bytes 8847360 | tf_op jit(solution)/shard_map/reduce_scatter | solution.py:169
  48.9 2.8 %copy-start.13 = (s32[1536]{0:T(1024)S(1)}, s32[1536]{0:T(1024)}, u32[]{:S(2)}) copy-start(s32[1536]{0:T(1024)} %param.10) | copy-start | bytes 18436
  98.7 2.9 %copy-start = (f32[384,4,2,1,64]{0,4,2,1,3:T(8,128)}, f32[384,4,2,1,64]{0,4,2,1,3:T(8,128)S(1)}, u32[]{:S(2)}) copy-start(f32[384,4,2,1,64]{0,4,2,1,3:T(8,128)S(1)} %slice.88) | copy-start | bytes 2359300
  107.8 2.7 copy-start.4
  110.6 6.3 %copy-start.2 = (f32[192,1280]{1,0:T(8,128)S(1)}, f32[192,1280]{1,0:T(8,128)}, u32[]{:S(2)}) copy-start(f32[192,1280]{1,0:T(8,128)} %pad.13.clone) | copy-start | bytes 2949124
  110.6 6.3 %copy-start.6 = (f32[8,64,128]{2,1,0:T(8,128)S(1)}, f32[8,64,128]{2,1,0:T(8,128)}, u32[]{:S(2)}) copy-start(f32[8,64,128]{2,1,0:T(8,128)} %get-tuple-element.19) | copy-start | bytes 786436
  120.8 73.0 %copy-start.7 = (f32[1536,384]{1,0:T(8,128)S(1)}, f32[1536,384]{1,0:T(8,128)}, u32[]{:S(2)}) copy-start(f32[1536,384]{1,0:T(8,128)} %all-gather.7.cloned.1.call-done) | copy-start | bytes 7077892
  120.8 118.8 %all-gather.11.cloned.1.call-start = ((), (), s32[]{:S(2)}) async-start(), calls=%async_computation.4 | async-start | bytes 2621440 | tf_op jit(solution)/shard_map/all_gather | solution.py:183
  200.3 4.3 %copy-start.8 = (f32[1,192,1280]{2,1,0:T(8,128)S(1)}, f32[1,192,1280]{2,1,0:T(8,128)}, u32[]{:S(2)}) copy-start(f32[1,192,1280]{2,1,0:T(8,128)} %reduce-scatter.2.cloned.1.call-done) | copy-start | bytes 2949124
  245.2 2.5 copy-start.12
  245.2 3.0 %copy-start.1 = (f32[2,64,9,128]{3,2,1,0:T(8,128)S(1)}, f32[2,64,9,128]{3,2,1,0:T(8,128)}, u32[]{:S(2)}) copy-start(f32[2,64,9,128]{3,2,1,0:T(8,128)} %neg.32) | copy-start | bytes 1769476
  247.6 0.7 copy-start.10
  248.3 16.4 %copy-start.5 = (f32[64,4,432]{2,1,0:T(4,128)S(1)}, f32[64,4,432]{2,1,0:T(4,128)}, u32[]{:S(2)}) copy-start(f32[64,4,432]{2,1,0:T(4,128)} %slice.100) | copy-start | bytes 1327108
  248.4 18.1 %copy-start.9 = (f32[1728,128]{1,0:T(8,128)S(1)}, f32[1728,128]{1,0:T(8,128)}, u32[]{:S(2)}) copy-start(f32[1728,128]{1,0:T(8,128)} %fusion.1) | copy-start | bytes 2654212
  248.4 18.1 %copy-start.14 = (f32[1,1,64,128]{3,2,1,0:T(8,128)S(1)}, f32[1,1,64,128]{3,2,1,0:T(8,128)}, u32[]{:S(2)}) copy-start(f32[1,1,64,128]{3,2,1,0:T(8,128)} %param.11) | copy-start | bytes 98308
Sparse Core Ops, SparseCore 0:
  10.4 31.5 all-gather.6
  48.4 45.9 all-gather.8
  121.0 68.2 reduce-scatter.1
  193.9 45.6 all-gather.10
